TPU v7x, 32 devices: a whole 2x2x4 slice. The times are simulated.
32 devices in a mesh: aux: 4 (over y, x), blk: 8 (over z, core).
Axes of the slice: x: 2, y: 2, z: 4, core: 2. Of those that a mesh axis runs over, the one named last changes fastest.
Arguments:
- integrals: bfloat16 [2048, 64, 1024], P(('aux', 'blk')), may hold values from -0.5 to 0.5
- metric: bfloat16 [2048, 512], P('aux'), may hold values from -1 to 2
- pair_list: int32 [15, 2], replicated, may hold values from 0 to 7, as said below
- aux_mask: int32 [16, 8], P('aux'), may hold values 0 or 1
Outputs:
- band_rows: float32 [8, 128, 640], P('blk', 'aux')
Inputs may be any that keep to these rules, and one draw needn't show every extreme that they name: `pair_list`: every pair (r, r) appears once; the other rows are distinct pairs (r, r + 1) or (r, r + 2) with both blocks below 8; 7 such rows.
All inputs are finite; a program needn't handle non-finite values. No bound on the sum of `aux_mask` on one device may be relied on, other than what follows from the above.
Results may differ from a plain program's by a relative error of at most 0.0015.
Values may be sent and summed in bfloat16 or wider, within the bound.
A program may use at most 128 MiB of HBM per device.

v0:
```python
import jax
import jax.numpy as jnp
from jax import lax
from jax.sharding import PartitionSpec as P

BS = 128
QB = 128
SPAN = 3


def from_behind(array, axis, by):
    peers = lax.axis_size(axis)
    pairs = [(i, i + by) for i in range(peers) if 0 <= i + by < peers]
    return lax.ppermute(array, axis, pairs)


def fit_block(metric, slab_piece, mask_rows):
    fitted = jnp.einsum("pq,qjn->pjn", metric, slab_piece, preferred_element_type=jnp.float32)
    return (fitted * mask_rows[:, None, None]).astype(jnp.bfloat16)


def local(integrals, metric, pair_list, aux_mask):
    block_count = aux_mask.shape[1]
    position = lax.axis_index("blk")
    block_ids = jnp.arange(block_count, dtype=jnp.int32)
    offsets = jnp.arange(SPAN, dtype=jnp.int32)
    col_gap = pair_list[:, 1] - pair_list[:, 0]
    hits = (pair_list[:, 0][:, None] == position) & (col_gap[:, None] == offsets[None, :])
    listed = jnp.sum(hits.astype(jnp.int32), axis=0)
    one_hot = (block_ids == position).astype(jnp.int32)
    column = jnp.sum(aux_mask * one_hot[None, :], axis=1)
    own_mask = jnp.repeat(column, QB).astype(jnp.float32)
    own_block = fit_block(
        metric, lax.all_to_all(integrals, "blk", split_axis=2, concat_axis=0, tiled=True), own_mask
    )
    partners = [own_block]
    current = own_block
    for turn_index in range(SPAN - 1):
        current = from_behind(current, "blk", -1)
        partners.append(current)
    flat_own = partners[0].reshape(-1, BS)

    def make_tile(partner):
        return lax.dot_general(
            flat_own,
            partner.reshape(-1, BS),
            (((0,), (0,)), ((), ())),
            preferred_element_type=jnp.float32,
        )

    tile_list = [
        make_tile(partners[offset]) * listed[offset].astype(jnp.float32) for offset in range(SPAN)
    ]
    upper_tiles = jnp.stack(tile_list)
    mirror_tiles = jnp.stack([jnp.transpose(tile_list[offset]) for offset in range(1, SPAN)])
    lower_tiles = []
    moving = mirror_tiles
    for turn_index in range(SPAN - 1):
        moving = from_behind(moving.astype(jnp.bfloat16), "blk", 1).astype(moving.dtype)
        lower_tiles.append(moving[0])
        moving = moving[1:]
    whole_band = jnp.concatenate(
        [jnp.stack([lower_tiles[SPAN - 2 - slot] for slot in range(SPAN - 1)]), upper_tiles], axis=0
    )
    band_parts = lax.psum_scatter(whole_band, "aux", scatter_dimension=1, tiled=True)
    pieces = [band_parts[slot] for slot in range(2 * SPAN - 1)]
    band_rows = jnp.concatenate(pieces, axis=1)
    return band_rows[None]


def solution(mesh):
    return jax.shard_map(
        local,
        mesh=mesh,
        in_specs=(P(("aux", "blk"), None, None), P("aux", None), P(), P("aux", None)),
        out_specs=P("blk", "aux", None),
        check_vma=False,
    )
```

profile of v0, /device:TPU:0, one launch (start us, length us, event | category | flops | bytes accessed | tf_op | source)
XLA Modules:
  0.0 535.0 jit_solution(6103885854642759354)
XLA Ops:
  6.5 0.0 copy-start
  6.5 24.0 %copy.18 = bf16[64,64,1024]{1,0,2:T(8,128)(2,1)} copy(bf16[64,64,1024]{2,1,0:T(8,128)(2,1)} %param.4) | data formatting | bytes 16777216 | tf_op args[0]
  30.5 16.9 %reshape.23 = bf16[8,2,262144]{2,1,0:T(2,128)(2,1)} reshape(bf16[1024,64,64]{2,1,0:T(8,128)(2,1)} %bitcast.79) | data formatting | bytes 16777216
  47.4 0.0 copy-start.4
  47.4 6.5 %all-to-all-start = ((bf16[8,2,262144]{2,1,0:T(2,128)(2,1)}), bf16[8,2,262144]{2,1,0:T(2,128)(2,1)}, u32[]{:S(2)}, u32[]{:S(2)}) async-start(bf16[8,2,262144]{2,1,0:T(2,128)(2,1)} %reshape.23), calls=%async_computation | async-start | bytes 16777216 | tf_op jit(solution)/shard_map/all_to_all | solution.py:34
  53.9 0.0 reduce-scatter.2.cloned.1.call-start
  54.0 0.0 copy-done.4
  54.0 0.1 multiply_reduce_fusion
  54.1 0.1 broadcast_bitcast_fusion
  54.2 183.7 %all-to-all-done = bf16[8,2,262144]{2,1,0:T(2,128)(2,1)} async-done(((bf16[8,2,262144]{2,1,0:T(2,128)(2,1)}), bf16[8,2,262144]{2,1,0:T(2,128)(2,1)}, u32[]{:S(2)}, u32[]{:S(2)}) %all-to-all-start) | async-done | bytes 8388640 | tf_op jit(solution)/shard_map/all_to_all | solution.py:34
  237.9 16.5 %reshape.24 = bf16[1024,64,64]{2,1,0:T(8,128)(2,1)} reshape(bf16[8,2,262144]{2,1,0:T(2,128)(2,1)} %all-to-all-done) | data formatting | bytes 16777216
  254.3 27.7 %copy.19 = bf16[64,64,8,128]{3,0,2,1:T(8,128)(2,1)} copy(bf16[64,64,8,128]{1,0,3,2:T(8,128)(2,1)} %bitcast.78) | data formatting | bytes 16777216 | tf_op jit(solution)/shard_map/all_to_all | solution.py:34
  282.1 0.0 copy-done
  282.1 0.0 copy-start.5
  282.1 8.1 %multiply_convert_fusion = bf16[512,64,128]{2,0,1:T(8,128)(2,1)S(1)} fusion(bf16[512,64,128]{2,0,1:T(8,128)(2,1)} %bitcast.80, f32[512]{0:T(512)S(1)} %broadcast_bitcast_fusion, bf16[512,512]{1,0:T(8,128)(2,1)S(1)} %copy-done), kind=kOutput, calls=%fused_computation | convolution fusion | flops 4303355904 | bytes 17303552 | tf_op jit(solution)/shard_map/pq,qjn->pjn/dot_general | solution.py:18
  290.2 0.0 copy-start.1
  290.2 1.3 collective-permute-start
  291.5 13.8 %collective-permute-done = bf16[512,64,128]{2,0,1:T(8,128)(2,1)S(1)} collective-permute-done((bf16[512,64,128]{2,0,1:T(8,128)(2,1)S(1)}, bf16[512,64,128]{2,0,1:T(8,128)(2,1)S(1)}, u32[]{:S(2)}, u32[]{:S(2)}) %collective-permute-start) | collective-permute-done | bytes 8388640 | tf_op jit(solution)/shard_map/ppermute | solution.py:14
  305.3 1.5 collective-permute-start.1
  306.7 0.0 copy-done.5
  306.8 0.1 convert_reduce_fusion
  306.9 0.7 fusion.7
  308.9 2.5 fusion.4
  311.4 87.7 %collective-permute-done.1 = bf16[512,64,128]{2,0,1:T(8,128)(2,1)S(1)} collective-permute-done((bf16[512,64,128]{2,0,1:T(8,128)(2,1)S(1)}, bf16[512,64,128]{2,0,1:T(8,128)(2,1)S(1)}, u32[]{:S(2)}, u32[]{:S(2)}) %collective-permute-start.1) | collective-permute-done | bytes 8388640 | tf_op jit(solution)/shard_map/ppermute | solution.py:14
  399.1 0.0 copy-done.1
  399.1 2.4 fusion.3
  401.5 82.1 %collective-permute-start.2 = (bf16[2,128,128]{1,2,0:T(8,128)(2,1)S(1)}, bf16[2,128,128]{1,2,0:T(8,128)(2,1)S(1)}, u32[]{:S(2)}, u32[]{:S(2)}) collective-permute-start(bf16[2,128,128]{1,2,0:T(8,128)(2,1)S(1)} %pad_maximum_fusion), channel_id=1, source_target_pairs={{0,1},{1,2},{2,3},{3,4},{4,5},{5,6},{6,7},{8,9},{9,10},{10,11},{11... | collective-permute-start | bytes 196616 | tf_op jit(solution)/shard_map/ppermute | solution.py:14
  483.6 0.9 collective-permute-done.2
  484.5 2.3 collective-permute-start.3
  487.5 0.1 copy.24
  487.6 0.1 collective-permute-done.3
  487.7 0.1 copy.23
  487.8 8.2 %fusion.2 = f32[5,128,128]{2,1,0:T(8,128)S(1)} fusion(f32[5,128,128]{2,1,0:T(8,128)S(1)} %constant_dynamic-update-slice_fusion, bf16[512,64,128]{2,0,1:T(8,128)(2,1)} %copy-done.1, f32[]{:T(128)} %bitcast.16), kind=kOutput, calls=%fused_computation.4 | convolution fusion | flops 1073758208 | bytes 16843264 | tf_op jit(solution)/shard_map/dot_general | solution.py:44
  496.0 0.0 copy-start.2
  496.0 0.7 copy-done.2
  496.7 0.0 reduce-scatter.2.cloned.1.call-update
  496.8 27.1 %reduce-scatter.2.cloned.1.call-done = f32[5,32,128]{2,1,0:T(8,128)} async-done(((f32[5,128,128]{2,1,0:T(8,128)}), f32[5,32,128]{2,1,0:T(8,128)}) %reduce-scatter.2.cloned.1.call-update) | async-done | bytes 81936 | tf_op jit(solution)/shard_map/reduce_scatter | solution.py:65
  523.9 0.7 constant_dynamic-update-slice_fusion.6
  524.6 0.7 constant_dynamic-update-slice_fusion.5
  525.4 0.7 constant_dynamic-update-slice_fusion.4
  526.1 0.7 constant_dynamic-update-slice_fusion.3
  526.8 0.7 constant_dynamic-update-slice_fusion.2
  527.5 0.0 copy-start.3
  527.5 0.6 copy-done.3
  (12 shorter events, 0.1 us)
Async XLA Ops:
  6.5 275.5 %copy-start = (bf16[512,512]{1,0:T(8,128)(2,1)S(1)}, bf16[512,512]{1,0:T(8,128)(2,1)}, u32[]{:S(2)}) copy-start(bf16[512,512]{1,0:T(8,128)(2,1)} %param.5) | copy-start | bytes 1572868
  47.4 6.5 %copy-start.4 = (s32[4,8]{1,0:T(4,128)S(1)}, s32[4,8]{1,0:T(4,128)}, u32[]{:S(2)}) copy-start(s32[4,8]{1,0:T(4,128)} %param.7) | copy-start | bytes 388
  47.4 190.4 %all-to-all-start = ((bf16[8,2,262144]{2,1,0:T(2,128)(2,1)}), bf16[8,2,262144]{2,1,0:T(2,128)(2,1)}, u32[]{:S(2)}, u32[]{:S(2)}) async-start(bf16[8,2,262144]{2,1,0:T(2,128)(2,1)} %reshape.23), calls=%async_computation | async-start | bytes 16777216 | tf_op jit(solution)/shard_map/all_to_all | solution.py:34
  53.9 470.0 %reduce-scatter.2.cloned.1.call-start = ((), (), s32[]{:S(2)}) async-start(), calls=%async_computation.2 | async-start | bytes 409600 | tf_op jit(solution)/shard_map/reduce_scatter | solution.py:65
  282.1 24.7 %copy-start.5 = (s32[15,2]{0,1:T(2,128)S(1)}, s32[15,2]{0,1:T(2,128)}, u32[]{:S(2)}) copy-start(s32[15,2]{0,1:T(2,128)} %param.6) | copy-start | bytes 364
  290.2 108.9 %copy-start.1 = (bf16[512,64,128]{2,0,1:T(8,128)(2,1)}, bf16[512,64,128]{2,0,1:T(8,128)(2,1)S(1)}, u32[]{:S(2)}) copy-start(bf16[512,64,128]{2,0,1:T(8,128)(2,1)S(1)} %multiply_convert_fusion) | copy-start | bytes 25165828
  290.2 15.1 %collective-permute-start = (bf16[512,64,128]{2,0,1:T(8,128)(2,1)S(1)}, bf16[512,64,128]{2,0,1:T(8,128)(2,1)S(1)}, u32[]{:S(2)}, u32[]{:S(2)}) collective-permute-start(bf16[512,64,128]{2,0,1:T(8,128)(2,1)S(1)} %multiply_convert_fusion), channel_id=1, source_target_pairs={{1,0},{2,1},{3,2},{4,3},{5,4},{6,5},{7,6},{9,8},{10,9},{11,10},{12... | collective-permute-start | bytes 25165832 | tf_op jit(solution)/shard_map/ppermute | solution.py:14
  305.3 93.8 %collective-permute-start.1 = (bf16[512,64,128]{2,0,1:T(8,128)(2,1)S(1)}, bf16[512,64,128]{2,0,1:T(8,128)(2,1)S(1)}, u32[]{:S(2)}, u32[]{:S(2)}) collective-permute-start(bf16[512,64,128]{2,0,1:T(8,128)(2,1)S(1)} %collective-permute-done), channel_id=1, source_target_pairs={{1,0},{2,1},{3,2},{4,3},{5,4},{6,5},{7,6},{9,8},{10,9},{11,10},{12... | collective-permute-start | bytes 25165832 | tf_op jit(solution)/shard_map/ppermute | solution.py:14
  401.5 83.0 %collective-permute-start.2 = (bf16[2,128,128]{1,2,0:T(8,128)(2,1)S(1)}, bf16[2,128,128]{1,2,0:T(8,128)(2,1)S(1)}, u32[]{:S(2)}, u32[]{:S(2)}) collective-permute-start(bf16[2,128,128]{1,2,0:T(8,128)(2,1)S(1)} %pad_maximum_fusion), channel_id=1, source_target_pairs={{0,1},{1,2},{2,3},{3,4},{4,5},{5,6},{6,7},{8,9},{9,10},{10,11},{11... | collective-permute-start | bytes 196616 | tf_op jit(solution)/shard_map/ppermute | solution.py:14
  484.5 3.2 collective-permute-start.3
  496.0 0.7 copy-start.2
  527.5 0.6 copy-start.3
Sparse Core Ops, SparseCore 0:
  496.9 26.9 reduce-scatter.1
where the time goes:
time: 537 us; the launch traced here: 535 us
  waiting for transfers between devices  313 us (58%)
  starting transfers between devices  93.7 us (17%)
  local copies, waits for them, and re-layouts  91 us (17%)
  matrix products  21.2 us (4%)
  between operations  15.5 us (3%)
    all_to_all x1, waiting for transfers between devices, local(): lax.all_to_all(integrals, 'blk', split_axis=2, concat_axis=0, tiled=True)  184 us
    ppermute x4, waiting for transfers between devices, from_behind(): return lax.ppermute(array, axis, pairs)  102 us
    ppermute x4, starting transfers between devices, from_behind(): return lax.ppermute(array, axis, pairs)  87.2 us
    unnamed x22, local copies, waits for them, and re-layouts  61.6 us
    all_to_all x1, local copies, waits for them, and re-layouts, local(): lax.all_to_all(integrals, 'blk', split_axis=2, concat_axis=0, tiled=True)  27.7 us
    reduce_scatter x1, waiting for transfers between devices, local(): lax.psum_scatter(whole_band, 'aux', scatter_dimension=1, tiled=True)  27.1 us
    dot_general x3, matrix products, make_tile(): lax.dot_general(flat_own, partner.reshape(-1, BS), (((0,), (0,)), ((), ()...  13.1 us
  transfers between devices with their start and end apart: 6, of which 6 were waited for; matrix products, arithmetic and copies ran while one was open for 1% of the time, Pallas kernels for 0%

commit v1 on v0

--- a/solution.py
+++ b/solution.py
@@ -1,11 +1,189 @@
+import functools
+
 import jax
 import jax.numpy as jnp
 from jax import lax
+from jax.experimental import pallas as pl
+from jax.experimental.pallas import tpu as pltpu
 from jax.sharding import PartitionSpec as P
 
 BS = 128
 QB = 128
 SPAN = 3
+SUB = 8
+MESH = pl.DeviceIdType.MESH
+
+
+def listed_of(pair_list, block_count):
+    block_ids = jnp.arange(block_count, dtype=jnp.int32)
+    offsets = jnp.arange(SPAN, dtype=jnp.int32)
+    col_gap = pair_list[:, 1] - pair_list[:, 0]
+    hits = (pair_list[:, 0][:, None, None] == block_ids[None, :, None]) & (
+        col_gap[:, None, None] == offsets[None, None, :]
+    )
+    return jnp.sum(hits.astype(jnp.int32), axis=0)
+
+
+def tile_kernel(
+    peers, blocks, depth, mask_ref, metric_ref, x_ref, out_ref,
+    slab, wide, ordered, fit_rows, fit_cols, send_sem, recv_sem, own_sem,
+):
+    me = lax.axis_index("blk")
+    rows = depth // peers
+
+    barrier = pltpu.get_barrier_semaphore()
+
+    def greet(off, carry):
+        pl.semaphore_signal(
+            barrier, inc=1, device_id={"blk": lax.rem(me + off, peers)}, device_id_type=MESH
+        )
+        return carry
+
+    lax.fori_loop(1, peers, greet, 0)
+    pl.semaphore_wait(barrier, peers - 1)
+
+    def source(block, target):
+        return x_ref.at[
+            :,
+            pl.ds(pl.multiple_of(target * SUB, SUB), SUB),
+            pl.ds(pl.multiple_of(block * BS, BS), BS),
+        ]
+
+    def landing(block, sender):
+        return slab.at[block, pl.ds(pl.multiple_of(sender * rows, rows), rows)]
+
+    def outgoing(block, off):
+        target = lax.rem(me + off, peers)
+        return pltpu.make_async_remote_copy(
+            src_ref=source(block, target),
+            dst_ref=landing(block, me),
+            send_sem=send_sem.at[block, off],
+            recv_sem=recv_sem.at[block, off],
+            device_id={"blk": target},
+            device_id_type=MESH,
+        )
+
+    def incoming(block, off):
+        sender = lax.rem(me - off + peers, peers)
+        return pltpu.make_async_remote_copy(
+            src_ref=source(block, me),
+            dst_ref=landing(block, sender),
+            send_sem=send_sem.at[block, off],
+            recv_sem=recv_sem.at[block, off],
+            device_id={"blk": sender},
+            device_id_type=MESH,
+        )
+
+    def own(block):
+        return pltpu.make_async_copy(source(block, me), landing(block, me), own_sem.at[block])
+
+    def launch(block, carry):
+        def one(off, inner):
+            outgoing(block, off).start()
+            return inner
+
+        lax.fori_loop(1, peers, one, 0)
+        own(block).start()
+        return carry
+
+    lax.fori_loop(0, blocks, launch, 0)
+
+    fit_cols[: (SPAN - 1) * BS, :] = jnp.zeros(((SPAN - 1) * BS, SUB * depth), jnp.bfloat16)
+
+    def step(block, carry):
+        def arrive(off, inner):
+            incoming(block, off).wait_recv()
+            return inner
+
+        lax.fori_loop(1, peers, arrive, 0)
+        own(block).wait()
+        wide[...] = slab[block].reshape(depth * SUB, BS).astype(jnp.float32)
+        for i in range(SUB):
+            ordered[:, i * BS : (i + 1) * BS] = wide[pl.ds(i, depth, stride=SUB), :].astype(
+                jnp.bfloat16
+            )
+        for qb in range(depth // QB):
+            keep = mask_ref[qb, block].astype(jnp.float32)
+            fitted = jnp.dot(
+                metric_ref[qb * QB : (qb + 1) * QB, :],
+                ordered[...],
+                preferred_element_type=jnp.float32,
+            )
+            fitted = fitted * keep
+            for i in range(SUB):
+                piece = fitted[:, i * BS : (i + 1) * BS]
+                at = i * depth + qb * QB
+                fit_rows[at : at + QB, :] = piece.astype(jnp.bfloat16)
+                fit_cols[
+                    pl.ds(pl.multiple_of((block + SPAN - 1) * BS, BS), BS), at : at + QB
+                ] = piece.T.astype(jnp.bfloat16)
+        out_ref[block] = jnp.dot(
+            fit_cols[pl.ds(pl.multiple_of(block * BS, BS), SPAN * BS), :],
+            fit_rows[...],
+            preferred_element_type=jnp.float32,
+        )
+        return carry
+
+    lax.fori_loop(0, blocks, step, 0)
+
+    def settle(block, carry):
+        def one(off, inner):
+            outgoing(block, off).wait_send()
+            return inner
+
+        lax.fori_loop(1, peers, one, 0)
+        return carry
+
+    lax.fori_loop(0, blocks, settle, 0)
+
+
+def partial_tiles(integrals, metric, aux_mask, peers):
+    depth = metric.shape[1]
+    blocks = aux_mask.shape[1]
+    return pl.pallas_call(
+        functools.partial(tile_kernel, peers, blocks, depth),
+        out_shape=jax.ShapeDtypeStruct((blocks, SPAN * BS, BS), jnp.float32),
+        in_specs=[
+            pl.BlockSpec(memory_space=pltpu.SMEM),
+            pl.BlockSpec(memory_space=pltpu.VMEM),
+            pl.BlockSpec(memory_space=pl.ANY),
+        ],
+        out_specs=pl.BlockSpec(memory_space=pltpu.VMEM),
+        scratch_shapes=[
+            pltpu.VMEM((blocks, depth, SUB, BS), jnp.bfloat16),
+            pltpu.VMEM((depth * SUB, BS), jnp.float32),
+            pltpu.VMEM((depth, SUB * BS), jnp.bfloat16),
+            pltpu.VMEM((SUB * depth, BS), jnp.bfloat16),
+            pltpu.VMEM(((blocks + SPAN - 1) * BS, SUB * depth), jnp.bfloat16),
+            pltpu.SemaphoreType.DMA((blocks, peers)),
+            pltpu.SemaphoreType.DMA((blocks, peers)),
+            pltpu.SemaphoreType.DMA((blocks,)),
+        ],
+        compiler_params=pltpu.CompilerParams(
+            collective_id=0, has_side_effects=True, vmem_limit_bytes=60 * 1024 * 1024
+        ),
+    )(aux_mask, metric, integrals)
+
+
+def by_orbital(integrals, metric, pair_list, aux_mask):
+    peers = lax.axis_size("blk")
+    blocks = aux_mask.shape[1]
+    listed = listed_of(pair_list, blocks).astype(jnp.float32)
+    parts = partial_tiles(integrals, metric, aux_mask, peers)
+    parts = parts.reshape(blocks, SPAN, BS, BS)
+    pieces = []
+    for slot in range(2 * SPAN - 1):
+        offset = slot - (SPAN - 1)
+        if offset < 0:
+            weight = jnp.pad(listed[: blocks + offset, -offset], (-offset, 0))
+            tile = jnp.swapaxes(parts[:, SPAN - 1 + offset], 1, 2)
+        else:
+            weight = listed[:, offset]
+            tile = jnp.pad(parts[offset:, SPAN - 1 - offset], ((0, offset), (0, 0), (0, 0)))
+        pieces.append(tile * weight[:, None, None])
+    band = jnp.concatenate(pieces, axis=2)
+    band = lax.psum_scatter(band, "aux", scatter_dimension=1, tiled=True)
+    return lax.psum_scatter(band, "blk", scatter_dimension=0, tiled=True)
 
 
 def from_behind(array, axis, by):
@@ -19,7 +197,7 @@
     return (fitted * mask_rows[:, None, None]).astype(jnp.bfloat16)
 
 
-def local(integrals, metric, pair_list, aux_mask):
+def by_block(integrals, metric, pair_list, aux_mask):
     block_count = aux_mask.shape[1]
     position = lax.axis_index("blk")
     block_ids = jnp.arange(block_count, dtype=jnp.int32)
@@ -68,6 +246,15 @@
     return band_rows[None]
 
 
+def local(integrals, metric, pair_list, aux_mask):
+    peers = lax.axis_size("blk")
+    blocks = aux_mask.shape[1]
+    whole_tiles = integrals.shape[1] == SUB * peers and blocks == peers
+    if whole_tiles:
+        return by_orbital(integrals, metric, pair_list, aux_mask)
+    return by_block(integrals, metric, pair_list, aux_mask)
+
+
 def solution(mesh):
     return jax.shard_map(
         local,

time: 537 us -> 291 us (0.54)
  waiting for transfers between devices: 313 us -> 81.5 us
  Pallas kernels: 0 us -> 184 us
  starting transfers between devices: 93.7 us -> 0.04 us
  local copies, waits for them, and re-layouts: 91 us -> 5.75 us
  matrix products: 21.2 us -> 0 us
  other arithmetic: 0.28 us -> 5.72 us
    pallas_call x0 -> x1, Pallas kernels: none -> 184 us  [partial_tiles(): pl.pallas_call(functools.partial(tile_kernel, peers, blocks, depth), out_...]
    all_to_all x1 -> x0, waiting for transfers between devices: 184 us -> none  [local(): lax.all_to_all(integrals, 'blk', split_axis=2, concat_axis=0, tiled=True)]
    ppermute x4 -> x0, waiting for transfers between devices: 102 us -> none  [from_behind(): return lax.ppermute(array, axis, pairs)]
    ppermute x4 -> x0, starting transfers between devices: 87.2 us -> none  [from_behind(): return lax.ppermute(array, axis, pairs)]
    unnamed x22 -> x6, local copies, waits for them, and re-layouts: 61.6 us -> 0.4 us
    reduce_scatter x1 -> x2, waiting for transfers between devices: 27.1 us -> 81.5 us  [the longest x1 47.6 us: by_orbital(): band = lax.psum_scatter(band, 'aux', scatter_dimension=1, tiled=True)]
    all_to_all x1 -> x0, local copies, waits for them, and re-layouts: 27.7 us -> none  [local(): lax.all_to_all(integrals, 'blk', split_axis=2, concat_axis=0, tiled=True)]
    dot_general x4 -> x0, matrix products: 21.2 us -> none  [the longest x3 13.1 us: make_tile(): lax.dot_general(flat_own, partner.reshape(-1, BS), (((0,), (0,)), ((), ()...]
  transfers between devices with their start and end apart: 6 -> 2, of which waited for: 6 -> 2; matrix products, arithmetic and copies ran while one was open for 1% -> 0% of each run, Pallas kernels for 0% -> 0%
where the time goes in v1:
time: 291 us
  Pallas kernels  184 us (63%)
  waiting for transfers between devices  81.5 us (28%)
  between operations  13.5 us (5%)
  local copies, waits for them, and re-layouts  5.75 us (2%)
  other arithmetic  5.72 us (2%)
    pallas_call x1, Pallas kernels, partial_tiles(): pl.pallas_call(functools.partial(tile_kernel, peers, blocks, depth), out_...  184 us
    reduce_scatter x1, waiting for transfers between devices, by_orbital(): band = lax.psum_scatter(band, 'aux', scatter_dimension=1, tiled=True)  47.6 us
    reduce_scatter x1, waiting for transfers between devices, by_orbital(): return lax.psum_scatter(band, 'blk', scatter_dimension=0, tiled=True)  33.9 us
  transfers between devices with their start and end apart: 2, of which 2 were waited for; matrix products, arithmetic and copies ran while one was open for 0% of the time, Pallas kernels for 0%

profile of v1, /device:TPU:0, one launch (start us, length us, event | category | flops | bytes accessed | tf_op | source)
XLA Modules:
  0.0 290.9 jit_solution(12969930703225242475)
XLA Ops:
  6.5 0.0 reduce-scatter.3.cloned.1.call-start
  6.5 0.7 slice_bitcast_fusion.8
  7.2 0.8 bitcast_subtract_fusion
  8.0 0.1 convert_reduce_fusion
  8.1 0.5 slice_bitcast_fusion.7
  8.7 184.5 %shard_map.46 = f32[8,384,128]{2,1,0:T(8,128)} custom-call(s32[4,8]{1,0:T(4,128)} %mask_ref.1, bf16[512,512]{1,0:T(8,128)(2,1)} %metric_ref.1, bf16[64,64,1024]{2,1,0:T(8,128)(2,1)} %x_ref.1), custom_call_target="tpu_custom_call" | custom-call | tf_op jit(solution)/shard_map/pallas_call | solution.py:143
  193.1 0.0 copy-start
  193.2 1.4 fusion.2
  194.6 1.8 slice_bitcast_fusion.1
  196.4 0.0 copy-done
  196.4 0.2 copy.15
  196.7 0.2 copy.16
  196.9 0.0 copy-start.1
  196.9 0.8 pad.16
  197.7 0.1 pad.17
  197.7 1.0 bitcast_dynamic-update-slice_fusion.1
  198.7 1.0 bitcast_dynamic-update-slice_fusion
  199.7 0.9 fusion.1
  200.6 0.0 copy-done.1
  200.6 1.0 multiply_dynamic-update-slice_fusion.1
  201.6 1.0 multiply_dynamic-update-slice_fusion
  202.5 0.0 reduce-scatter.3.cloned.1.call-update
  202.6 0.0 reduce-scatter.5.cloned.1.call-start
  202.6 47.6 %reduce-scatter.3.cloned.1.call-done = f32[8,32,640]{2,1,0:T(8,128)} async-done(((f32[8,128,640]{2,1,0:T(8,128)}), f32[8,32,640]{2,1,0:T(8,128)}) %reduce-scatter.3.cloned.1.call-update) | async-done | bytes 655376 | tf_op jit(solution)/shard_map/reduce_scatter | solution.py:185
  250.2 0.0 reduce-scatter.5.cloned.1.call-update
  250.2 33.9 %reduce-scatter.5.cloned.1.call-done = f32[1,32,640]{2,1,0:T(8,128)} async-done(((f32[8,32,640]{2,1,0:T(8,128)}), f32[1,32,640]{2,1,0:T(8,128)}) %reduce-scatter.5.cloned.1.call-update) | async-done | bytes 81936 | tf_op jit(solution)/shard_map/reduce_scatter | solution.py:186
  (6 shorter events, 0.1 us)
Async XLA Ops:
  6.5 243.6 %reduce-scatter.3.cloned.1.call-start = ((), (), s32[]{:S(2)}) async-start(), calls=%async_computation.2 | async-start | bytes 3276800 | tf_op jit(solution)/shard_map/reduce_scatter | solution.py:185
  193.1 3.3 %copy-start = (f32[8,384,128]{2,1,0:T(8,128)S(1)}, f32[8,384,128]{2,1,0:T(8,128)}, u32[]{:S(2)}) copy-start(f32[8,384,128]{2,1,0:T(8,128)} %shard_map.46) | copy-start | bytes 4718596
  196.9 3.7 %copy-start.1 = (f32[7,128,128]{2,1,0:T(8,128)S(1)}, f32[7,128,128]{2,1,0:T(8,128)}, u32[]{:S(2)}) copy-start(f32[7,128,128]{2,1,0:T(8,128)} %slice_bitcast_fusion.1) | copy-start | bytes 1376260
  202.6 81.5 %reduce-scatter.5.cloned.1.call-start = ((), (), s32[]{:S(2)}) async-start(), calls=%async_computation.3 | async-start | bytes 737280 | tf_op jit(solution)/shard_map/reduce_scatter | solution.py:186
Sparse Core Ops, SparseCore 0:
  202.7 47.4 reduce-scatter.2
  252.4 31.6 reduce-scatter.4

commit v2 on v1

--- a/solution.py
+++ b/solution.py
@@ -11,27 +11,29 @@
 QB = 128
 SPAN = 3
 SUB = 8
+PAIR = 2
 MESH = pl.DeviceIdType.MESH
 
 
-def listed_of(pair_list, block_count):
-    block_ids = jnp.arange(block_count, dtype=jnp.int32)
-    offsets = jnp.arange(SPAN, dtype=jnp.int32)
-    col_gap = pair_list[:, 1] - pair_list[:, 0]
-    hits = (pair_list[:, 0][:, None, None] == block_ids[None, :, None]) & (
-        col_gap[:, None, None] == offsets[None, None, :]
-    )
-    return jnp.sum(hits.astype(jnp.int32), axis=0)
-
-
 def tile_kernel(
-    peers, blocks, depth, mask_ref, metric_ref, x_ref, out_ref,
-    slab, wide, ordered, fit_rows, fit_cols, send_sem, recv_sem, own_sem,
+    peers, domains, blocks, depth, mask_ref, pairs_ref, metric_ref, x_ref, out_ref,
+    slab, wide, ordered, fit_rows, fit_cols, piece_out, piece_in, sum_out, sum_in, weights,
+    send_sem, recv_sem, own_sem, piece_send, piece_recv, sum_send, sum_recv,
 ):
     me = lax.axis_index("blk")
+    domain = lax.axis_index("aux")
     rows = depth // peers
+    group = domains * PAIR
+    strip = BS // group
+    pair_base = (me // PAIR) * PAIR
+    place = domain * PAIR + lax.rem(me, PAIR)
+    slots = 2 * SPAN - 1
 
     barrier = pltpu.get_barrier_semaphore()
+
+    def member(off):
+        other = lax.rem(place + off, group)
+        return {"aux": other // PAIR, "blk": pair_base + lax.rem(other, PAIR)}
 
     def greet(off, carry):
         pl.semaphore_signal(
@@ -40,7 +42,15 @@
         return carry
 
     lax.fori_loop(1, peers, greet, 0)
-    pl.semaphore_wait(barrier, peers - 1)
+    for turn in range(1, domains):
+        for core in range(PAIR):
+            pl.semaphore_signal(
+                barrier,
+                inc=1,
+                device_id={"aux": lax.rem(domain + turn, domains), "blk": pair_base + core},
+                device_id_type=MESH,
+            )
+    pl.semaphore_wait(barrier, peers - 1 + (domains - 1) * PAIR)
 
     def source(block, target):
         return x_ref.at[
@@ -88,9 +98,96 @@
 
     lax.fori_loop(0, blocks, launch, 0)
 
+    for slot in range(slots):
+        gap = abs(slot - (SPAN - 1))
+        row = me if slot >= SPAN - 1 else me - gap
+        count = jnp.int32(0)
+        for index in range(pairs_ref.shape[0]):
+            first = pairs_ref[index, 0]
+            hit = (first == row) & (pairs_ref[index, 1] - first == gap)
+            count = count + hit.astype(jnp.int32)
+        weights[slot] = count.astype(jnp.float32)
+
     fit_cols[: (SPAN - 1) * BS, :] = jnp.zeros(((SPAN - 1) * BS, SUB * depth), jnp.bfloat16)
+    for gap in range(1, SPAN):
+
+        @pl.when(me + gap >= blocks)
+        def _():
+            sum_in[:, SPAN - 1 + gap] = jnp.zeros((peers, strip, BS), jnp.float32)
+
+    def piece_to(block, off):
+        return pltpu.make_async_remote_copy(
+            src_ref=piece_out.at[block, lax.rem(place + off, group)],
+            dst_ref=piece_in.at[block, place],
+            send_sem=piece_send.at[block, off],
+            recv_sem=piece_recv.at[block, off],
+            device_id=member(off),
+            device_id_type=MESH,
+        )
+
+    def piece_from(block, off):
+        sender = lax.rem(place - off + group, group)
+        return pltpu.make_async_remote_copy(
+            src_ref=piece_out.at[block, sender],
+            dst_ref=piece_in.at[block, sender],
+            send_sem=piece_send.at[block, off],
+            recv_sem=piece_recv.at[block, off],
+            device_id=member(group - off),
+            device_id_type=MESH,
+        )
+
+    def span_of(gap):
+        return pl.ds(0, SPAN) if gap == 0 else pl.ds(SPAN - 1 + gap, 1)
+
+    def sum_to(block, gap):
+        return pltpu.make_async_remote_copy(
+            src_ref=sum_out.at[block, span_of(gap)],
+            dst_ref=sum_in.at[me, span_of(gap)],
+            send_sem=sum_send.at[block, gap],
+            recv_sem=sum_recv.at[me, gap],
+            device_id={"blk": block - gap},
+            device_id_type=MESH,
+        )
+
+    def sum_from(sender, gap):
+        return pltpu.make_async_remote_copy(
+            src_ref=sum_out.at[0, span_of(gap)],
+            dst_ref=sum_in.at[sender, span_of(gap)],
+            send_sem=sum_send.at[0, gap],
+            recv_sem=sum_recv.at[sender, gap],
+            device_id={"blk": sender},
+            device_id_type=MESH,
+        )
+
+    def pass_on(block):
+        def arrive(off, inner):
+            piece_from(block, off).wait_recv()
+            return inner
+
+        lax.fori_loop(1, group, arrive, 0)
+        total = piece_out[block, place]
+        for off in range(1, group):
+            total = total + piece_in[block, lax.rem(place + off, group)]
+        sum_out[block] = total
+        for gap in range(SPAN):
+            owner = block - gap
+
+            @pl.when((owner >= 0) & (owner != me))
+            def _():
+                sum_to(block, gap).start()
+
+            @pl.when(owner == me)
+            def _():
+                if gap == 0:
+                    sum_in[me, :SPAN] = total[:SPAN]
+                else:
+                    sum_in[me, SPAN - 1 + gap] = total[SPAN - 1 + gap]
 
     def step(block, carry):
+        @pl.when(block > 0)
+        def _():
+            pass_on(block - 1)
+
         def arrive(off, inner):
             incoming(block, off).wait_recv()
             return inner
@@ -117,33 +214,83 @@
                 fit_cols[
                     pl.ds(pl.multiple_of((block + SPAN - 1) * BS, BS), BS), at : at + QB
                 ] = piece.T.astype(jnp.bfloat16)
-        out_ref[block] = jnp.dot(
+        tiles = jnp.dot(
             fit_cols[pl.ds(pl.multiple_of(block * BS, BS), SPAN * BS), :],
             fit_rows[...],
             preferred_element_type=jnp.float32,
         )
+        for gap in range(SPAN):
+            at = (SPAN - 1 - gap) * BS
+            tile = tiles[at : at + BS, :]
+            piece_out[block, :, SPAN - 1 + gap] = tile.reshape(group, strip, BS)
+            if gap > 0:
+                piece_out[block, :, SPAN - 1 - gap] = tile.T.reshape(group, strip, BS)
+
+        def one(off, inner):
+            piece_to(block, off).start()
+            return inner
+
+        lax.fori_loop(1, group, one, 0)
         return carry
 
     lax.fori_loop(0, blocks, step, 0)
+    pass_on(blocks - 1)
+
+    for gap in range(SPAN):
+
+        @pl.when(me + gap < blocks)
+        def _():
+            def arrive(off, inner):
+                sum_from(lax.rem(me + off, peers), gap).wait_recv()
+                return inner
+
+            lax.fori_loop(1, peers, arrive, 0)
+
+    for core in range(PAIR):
+        for slot in range(slots):
+            total = sum_in[core, slot]
+            for turn in range(1, peers // PAIR):
+                total = total + sum_in[turn * PAIR + core, slot]
+            out_ref[0, core * strip : (core + 1) * strip, slot * BS : (slot + 1) * BS] = (
+                total * weights[slot]
+            )
 
     def settle(block, carry):
         def one(off, inner):
             outgoing(block, off).wait_send()
             return inner
 
+        def two(off, inner):
+            piece_to(block, off).wait_send()
+            return inner
+
         lax.fori_loop(1, peers, one, 0)
+        lax.fori_loop(1, group, two, 0)
+        for gap in range(SPAN):
+            owner = block - gap
+
+            @pl.when((owner >= 0) & (owner != me))
+            def _():
+                sum_to(block, gap).wait_send()
+
         return carry
 
     lax.fori_loop(0, blocks, settle, 0)
 
 
-def partial_tiles(integrals, metric, aux_mask, peers):
+def by_orbital(integrals, metric, pair_list, aux_mask):
+    peers = lax.axis_size("blk")
+    domains = lax.axis_size("aux")
     depth = metric.shape[1]
     blocks = aux_mask.shape[1]
+    group = domains * PAIR
+    slots = 2 * SPAN - 1
+    strip = BS // group
     return pl.pallas_call(
-        functools.partial(tile_kernel, peers, blocks, depth),
-        out_shape=jax.ShapeDtypeStruct((blocks, SPAN * BS, BS), jnp.float32),
+        functools.partial(tile_kernel, peers, domains, blocks, depth),
+        out_shape=jax.ShapeDtypeStruct((1, BS // domains, slots * BS), jnp.float32),
         in_specs=[
+            pl.BlockSpec(memory_space=pltpu.SMEM),
             pl.BlockSpec(memory_space=pltpu.SMEM),
             pl.BlockSpec(memory_space=pltpu.VMEM),
             pl.BlockSpec(memory_space=pl.ANY),
@@ -155,35 +302,23 @@
             pltpu.VMEM((depth, SUB * BS), jnp.bfloat16),
             pltpu.VMEM((SUB * depth, BS), jnp.bfloat16),
             pltpu.VMEM(((blocks + SPAN - 1) * BS, SUB * depth), jnp.bfloat16),
+            pltpu.VMEM((blocks, group, slots, strip, BS), jnp.float32),
+            pltpu.VMEM((blocks, group, slots, strip, BS), jnp.float32),
+            pltpu.VMEM((blocks, slots, strip, BS), jnp.float32),
+            pltpu.VMEM((peers, slots, strip, BS), jnp.float32),
+            pltpu.SMEM((slots,), jnp.float32),
             pltpu.SemaphoreType.DMA((blocks, peers)),
             pltpu.SemaphoreType.DMA((blocks, peers)),
             pltpu.SemaphoreType.DMA((blocks,)),
+            pltpu.SemaphoreType.DMA((blocks, group)),
+            pltpu.SemaphoreType.DMA((blocks, group)),
+            pltpu.SemaphoreType.DMA((blocks, SPAN)),
+            pltpu.SemaphoreType.DMA((peers, SPAN)),
         ],
         compiler_params=pltpu.CompilerParams(
             collective_id=0, has_side_effects=True, vmem_limit_bytes=60 * 1024 * 1024
         ),
-    )(aux_mask, metric, integrals)
-
-
-def by_orbital(integrals, metric, pair_list, aux_mask):
-    peers = lax.axis_size("blk")
-    blocks = aux_mask.shape[1]
-    listed = listed_of(pair_list, blocks).astype(jnp.float32)
-    parts = partial_tiles(integrals, metric, aux_mask, peers)
-    parts = parts.reshape(blocks, SPAN, BS, BS)
-    pieces = []
-    for slot in range(2 * SPAN - 1):
-        offset = slot - (SPAN - 1)
-        if offset < 0:
-            weight = jnp.pad(listed[: blocks + offset, -offset], (-offset, 0))
-            tile = jnp.swapaxes(parts[:, SPAN - 1 + offset], 1, 2)
-        else:
-            weight = listed[:, offset]
-            tile = jnp.pad(parts[offset:, SPAN - 1 - offset], ((0, offset), (0, 0), (0, 0)))
-        pieces.append(tile * weight[:, None, None])
-    band = jnp.concatenate(pieces, axis=2)
-    band = lax.psum_scatter(band, "aux", scatter_dimension=1, tiled=True)
-    return lax.psum_scatter(band, "blk", scatter_dimension=0, tiled=True)
+    )(aux_mask, pair_list, metric, integrals)
 
 
 def from_behind(array, axis, by):
@@ -249,7 +384,8 @@
 def local(integrals, metric, pair_list, aux_mask):
     peers = lax.axis_size("blk")
     blocks = aux_mask.shape[1]
-    whole_tiles = integrals.shape[1] == SUB * peers and blocks == peers
+    strips = BS % (8 * PAIR * lax.axis_size("aux")) == 0 and peers % PAIR == 0
+    whole_tiles = integrals.shape[1] == SUB * peers and blocks == peers and strips
     if whole_tiles:
         return by_orbital(integrals, metric, pair_list, aux_mask)
     return by_block(integrals, metric, pair_list, aux_mask)

time: 291 us -> 205 us (0.70)
  waiting for transfers between devices: 81.5 us -> 0 us
  Pallas kernels: 184 us -> 199 us
  between operations: 13.5 us -> 0.01 us
  other arithmetic: 5.72 us -> 0 us
    reduce_scatter x2 -> x0, waiting for transfers between devices: 81.5 us -> none  [the longest x1 47.6 us: by_orbital(): band = lax.psum_scatter(band, 'aux', scatter_dimension=1, tiled=True)]
    pallas_call x1, Pallas kernels: 184 us -> 199 us  [by_orbital(): pl.pallas_call(functools.partial(tile_kernel, peers, domains, blocks, dep...]
    unnamed x4 -> x0, other arithmetic: 3.83 us -> none
  transfers between devices with their start and end apart: 2 -> 0, of which waited for: 2 -> 0; matrix products, arithmetic and copies ran while one was open for 0% -> 0% of each run, Pallas kernels for 0% -> 0%
where the time goes in v2:
time: 205 us; the launch traced here: 202 us
  Pallas kernels  199 us (97%)
  local copies, waits for them, and re-layouts  2.89 us (1%)
    pallas_call x1, Pallas kernels, by_orbital(): pl.pallas_call(functools.partial(tile_kernel, peers, domains, blocks, dep...  199 us

profile of v2, /device:TPU:0, one launch (start us, length us, event | category | flops | bytes accessed | tf_op | source)
XLA Modules:
  0.0 202.2 jit_solution(17311038361510858643)
XLA Ops:
  0.0 1.4 copy.5.pairs_ref
  1.4 199.3 %shard_map.46 = f32[1,32,640]{2,1,0:T(8,128)} custom-call(s32[4,8]{1,0:T(4,128)} %mask_ref.1, s32[15,2]{1,0:T(8,128)} %copy.5.pairs_ref, bf16[512,512]{1,0:T(8,128)(2,1)} %metric_ref.1, bf16[64,64,1024]{2,1,0:T(8,128)(2,1)} %x_ref.1), custom_call_target="tpu_custom_call" | custom-call | tf_op jit(solution)/shard_map/pallas_call | solution.py:289
  200.7 1.5 copy.7

commit v3 on v2

--- a/solution.py
+++ b/solution.py
@@ -16,9 +16,10 @@
 
 
 def tile_kernel(
-    peers, domains, blocks, depth, mask_ref, pairs_ref, metric_ref, x_ref, out_ref,
+    peers, domains, blocks, depth, mask_hbm, pairs_hbm, metric_hbm, x_ref, out_ref,
+    mask_ref, pairs_ref, metric_ref,
     slab, wide, ordered, fit_rows, fit_cols, piece_out, piece_in, sum_out, sum_in, weights,
-    send_sem, recv_sem, own_sem, piece_send, piece_recv, sum_send, sum_recv,
+    send_sem, recv_sem, own_sem, piece_send, piece_recv, sum_send, sum_recv, load_sem,
 ):
     me = lax.axis_index("blk")
     domain = lax.axis_index("aux")
@@ -29,6 +30,13 @@
     place = domain * PAIR + lax.rem(me, PAIR)
     slots = 2 * SPAN - 1
 
+    loads = [
+        pltpu.make_async_copy(mask_hbm, mask_ref, load_sem.at[0]),
+        pltpu.make_async_copy(pairs_hbm, pairs_ref, load_sem.at[1]),
+        pltpu.make_async_copy(metric_hbm, metric_ref, load_sem.at[2]),
+    ]
+    for load in loads:
+        load.start()
     barrier = pltpu.get_barrier_semaphore()
 
     def member(off):
@@ -98,13 +106,15 @@
 
     lax.fori_loop(0, blocks, launch, 0)
 
+    for load in loads:
+        load.wait()
     for slot in range(slots):
         gap = abs(slot - (SPAN - 1))
         row = me if slot >= SPAN - 1 else me - gap
         count = jnp.int32(0)
-        for index in range(pairs_ref.shape[0]):
-            first = pairs_ref[index, 0]
-            hit = (first == row) & (pairs_ref[index, 1] - first == gap)
+        for index in range(pairs_ref.shape[1]):
+            first = pairs_ref[0, index]
+            hit = (first == row) & (pairs_ref[1, index] - first == gap)
             count = count + hit.astype(jnp.int32)
         weights[slot] = count.astype(jnp.float32)
 
@@ -183,6 +193,14 @@
                 else:
                     sum_in[me, SPAN - 1 + gap] = total[SPAN - 1 + gap]
 
+    def reorder(block, sender):
+        span = pl.ds(pl.multiple_of(sender * rows, rows), rows)
+        wide[...] = slab[block, span].reshape(rows * SUB, BS).astype(jnp.float32)
+        for i in range(SUB):
+            ordered[span, i * BS : (i + 1) * BS] = wide[pl.ds(i, rows, stride=SUB), :].astype(
+                jnp.bfloat16
+            )
+
     def step(block, carry):
         @pl.when(block > 0)
         def _():
@@ -190,15 +208,12 @@
 
         def arrive(off, inner):
             incoming(block, off).wait_recv()
-            return inner
-
+            reorder(block, lax.rem(me - off + peers, peers))
+            return inner
+
+        own(block).wait()
+        reorder(block, me)
         lax.fori_loop(1, peers, arrive, 0)
-        own(block).wait()
-        wide[...] = slab[block].reshape(depth * SUB, BS).astype(jnp.float32)
-        for i in range(SUB):
-            ordered[:, i * BS : (i + 1) * BS] = wide[pl.ds(i, depth, stride=SUB), :].astype(
-                jnp.bfloat16
-            )
         for qb in range(depth // QB):
             keep = mask_ref[qb, block].astype(jnp.float32)
             fitted = jnp.dot(
@@ -206,14 +221,14 @@
                 ordered[...],
                 preferred_element_type=jnp.float32,
             )
-            fitted = fitted * keep
+            fitted = (fitted * keep).astype(jnp.bfloat16)
             for i in range(SUB):
                 piece = fitted[:, i * BS : (i + 1) * BS]
                 at = i * depth + qb * QB
-                fit_rows[at : at + QB, :] = piece.astype(jnp.bfloat16)
+                fit_rows[at : at + QB, :] = piece
                 fit_cols[
                     pl.ds(pl.multiple_of((block + SPAN - 1) * BS, BS), BS), at : at + QB
-                ] = piece.T.astype(jnp.bfloat16)
+                ] = piece.T
         tiles = jnp.dot(
             fit_cols[pl.ds(pl.multiple_of(block * BS, BS), SPAN * BS), :],
             fit_rows[...],
@@ -290,15 +305,18 @@
         functools.partial(tile_kernel, peers, domains, blocks, depth),
         out_shape=jax.ShapeDtypeStruct((1, BS // domains, slots * BS), jnp.float32),
         in_specs=[
-            pl.BlockSpec(memory_space=pltpu.SMEM),
-            pl.BlockSpec(memory_space=pltpu.SMEM),
-            pl.BlockSpec(memory_space=pltpu.VMEM),
+            pl.BlockSpec(memory_space=pl.ANY),
+            pl.BlockSpec(memory_space=pl.ANY),
+            pl.BlockSpec(memory_space=pl.ANY),
             pl.BlockSpec(memory_space=pl.ANY),
         ],
         out_specs=pl.BlockSpec(memory_space=pltpu.VMEM),
         scratch_shapes=[
+            pltpu.SMEM(aux_mask.shape, jnp.int32),
+            pltpu.SMEM(pair_list.shape[::-1], jnp.int32),
+            pltpu.VMEM(metric.shape, jnp.bfloat16),
             pltpu.VMEM((blocks, depth, SUB, BS), jnp.bfloat16),
-            pltpu.VMEM((depth * SUB, BS), jnp.float32),
+            pltpu.VMEM((depth // peers * SUB, BS), jnp.float32),
             pltpu.VMEM((depth, SUB * BS), jnp.bfloat16),
             pltpu.VMEM((SUB * depth, BS), jnp.bfloat16),
             pltpu.VMEM(((blocks + SPAN - 1) * BS, SUB * depth), jnp.bfloat16),
@@ -314,11 +332,12 @@
             pltpu.SemaphoreType.DMA((blocks, group)),
             pltpu.SemaphoreType.DMA((blocks, SPAN)),
             pltpu.SemaphoreType.DMA((peers, SPAN)),
+            pltpu.SemaphoreType.DMA((3,)),
         ],
         compiler_params=pltpu.CompilerParams(
             collective_id=0, has_side_effects=True, vmem_limit_bytes=60 * 1024 * 1024
         ),
-    )(aux_mask, pair_list, metric, integrals)
+    )(aux_mask, pair_list.T, metric, integrals)
 
 
 def from_behind(array, axis, by):

time: 205 us -> 202 us (0.985)
  no operation moved by 1% of the time
where the time goes in v3:
time: 202 us; the launch traced here: 200 us
  Pallas kernels  198 us (98%)
    pallas_call x1, Pallas kernels, by_orbital(): pl.pallas_call(functools.partial(tile_kernel, peers, domains, blocks, dep...  198 us

profile of v3, /device:TPU:0, one launch (start us, length us, event | category | flops | bytes accessed | tf_op | source)
XLA Modules:
  0.0 199.8 jit_solution(3779793392729223504)
XLA Ops:
  0.0 198.2 %shard_map.46 = f32[1,32,640]{2,1,0:T(8,128)} custom-call(s32[4,8]{1,0:T(4,128)} %mask_hbm.1, s32[2,15]{1,0:T(2,128)} %bitcast.1, bf16[512,512]{1,0:T(8,128)(2,1)} %metric_hbm.1, bf16[64,64,1024]{2,1,0:T(8,128)(2,1)} %x_ref.1), custom_call_target="tpu_custom_call" | custom-call | tf_op jit(solution)/shard_map/pallas_call | solution.py:304
  198.2 1.5 copy.6

commit v4 on v3

--- a/solution.py
+++ b/solution.py
@@ -182,16 +182,22 @@
         for gap in range(SPAN):
             owner = block - gap
 
-            @pl.when((owner >= 0) & (owner != me))
-            def _():
-                sum_to(block, gap).start()
-
             @pl.when(owner == me)
             def _():
                 if gap == 0:
                     sum_in[me, :SPAN] = total[:SPAN]
                 else:
                     sum_in[me, SPAN - 1 + gap] = total[SPAN - 1 + gap]
+
+    def ship(block, carry):
+        for gap in range(SPAN):
+            owner = block - gap
+
+            @pl.when((owner >= 0) & (owner != me))
+            def _():
+                sum_to(block, gap).start()
+
+        return carry
 
     def reorder(block, sender):
         span = pl.ds(pl.multiple_of(sender * rows, rows), rows)
@@ -214,6 +220,11 @@
         own(block).wait()
         reorder(block, me)
         lax.fori_loop(1, peers, arrive, 0)
+
+        @pl.when(block == blocks - 1)
+        def _():
+            lax.fori_loop(0, blocks - 1, ship, 0)
+
         for qb in range(depth // QB):
             keep = mask_ref[qb, block].astype(jnp.float32)
             fitted = jnp.dot(
@@ -250,6 +261,7 @@
 
     lax.fori_loop(0, blocks, step, 0)
     pass_on(blocks - 1)
+    ship(blocks - 1, 0)
 
     for gap in range(SPAN):
 
@@ -291,6 +303,10 @@
         return carry
 
     lax.fori_loop(0, blocks, settle, 0)
+
+
+def in_hbm(operand):
+    return pltpu.with_memory_space_constraint(operand, pltpu.MemorySpace.HBM)
 
 
 def by_orbital(integrals, metric, pair_list, aux_mask):
@@ -335,9 +351,9 @@
             pltpu.SemaphoreType.DMA((3,)),
         ],
         compiler_params=pltpu.CompilerParams(
-            collective_id=0, has_side_effects=True, vmem_limit_bytes=60 * 1024 * 1024
+            collective_id=0, has_side_effects=True, vmem_limit_bytes=36 * 1024 * 1024
         ),
-    )(aux_mask, pair_list.T, metric, integrals)
+    )(*[in_hbm(operand) for operand in (aux_mask, pair_list.T, metric, integrals)])
 
 
 def from_behind(array, axis, by):

time: 202 us -> 200 us (0.990)
  no operation moved by 1% of the time
where the time goes in v4:
time: 200 us; the launch traced here: 198 us
  Pallas kernels  197 us (98%)
    pallas_call x1, Pallas kernels, by_orbital(): pl.pallas_call(functools.partial(tile_kernel, peers, domains, blocks, dep...  197 us

profile of v4, /device:TPU:0, one launch (start us, length us, event | category | flops | bytes accessed | tf_op | source)
XLA Modules:
  0.0 197.8 jit_solution(15017203077240436173)
XLA Ops:
  0.0 197.1 %shard_map.46 = f32[1,32,640]{2,1,0:T(8,128)S(1)} custom-call(s32[4,8]{1,0:T(4,128)} %mask_hbm.1, s32[2,15]{1,0:T(2,128)} %bitcast.1, bf16[512,512]{1,0:T(8,128)(2,1)} %metric_hbm.1, bf16[64,64,1024]{2,1,0:T(8,128)(2,1)} %x_ref.1), custom_call_target="tpu_custom_call" | custom-call | tf_op jit(solution)/shard_map/pallas_call | solution.py:320
  197.1 0.6 copy.6
